TPU v7x, 256 devices: a whole 4x4x8 slice. The times are simulated.
256 devices in a mesh: rows: 16 (over y, z_lo), cols: 16 (over x, z_hi, core).
Axes of the slice: x: 4, y: 4, z: 8 (z_hi: 2, z_lo: 4; z = z_hi * 4 + z_lo), core: 2. Of those that a mesh axis runs over, the one named last changes fastest.
Arguments:
- activations: bfloat16 [256, 256, 384], P('rows', 'cols'), may hold values from -6 to 6
- grad_out: bfloat16 [256, 256, 384], P('rows', 'cols'), may hold values from -6 to 6
- kernels: float32 [2, 7, 7, 384], replicated, may hold values from -0.875 to 0.875
- norm_gains: float32 [2, 384], replicated, may hold values from 0.5 to 1.5
- norm_shifts: float32 [2, 384], replicated, may hold values from -3 to 3
- w_in: bfloat16 [2, 384, 1536], replicated, may hold values from -0.3125 to 0.3125
- b_in: float32 [2, 1536], replicated, may hold values from -3 to 3
- w_out: bfloat16 [2, 384, 1536], replicated, may hold values from -0.15625 to 0.15625
Outputs:
- grad_in: bfloat16 [256, 256, 384], P('rows', 'cols')
- grad_kernels: float32 [2, 7, 7, 384], replicated
- grad_gains: float32 [2, 384], replicated
- grad_shifts: float32 [2, 384], replicated
- grad_b_in: float32 [2, 1536], replicated
- grad_w_in: float32 [2, 384, 1536], P(None, None, ('rows', 'cols'))
- grad_w_out: float32 [2, 384, 1536], P(None, None, ('rows', 'cols'))
All inputs are finite; a program needn't handle non-finite values.
Results may differ from a plain program's by a relative error of at most 0.017.
Values may be sent and summed in bfloat16 or wider, within the bound.
A program may use at most 128 MiB of HBM per device.

v0:
```python
import math
import jax
import jax.numpy as jnp
from jax import lax
from jax.sharding import PartitionSpec as P

EPSILON = 1e-06
ROOT_HALF = 0.7071067811865476
INV_ROOT_TAU = 0.3989422804014327


def with_halo(block, sides, width):
    for axis, dim in sides:
        count = lax.axis_size(axis)
        forward = [(i, i + 1) for i in range(count - 1)]
        backward = [(target, source) for source, target in forward]
        low = lax.ppermute(
            lax.slice_in_dim(block, block.shape[dim] - width, None, axis=dim), axis, forward
        )
        high = lax.ppermute(lax.slice_in_dim(block, 0, width, axis=dim), axis, backward)
        block = jnp.concatenate([low, block, high], axis=dim)
    return block


def gelu_parts(pre_act):
    normal_cdf = 0.5 * (1.0 + lax.erf(pre_act * ROOT_HALF))
    density = jnp.exp(-0.5 * pre_act * pre_act) * INV_ROOT_TAU
    return (pre_act * normal_cdf, normal_cdf + pre_act * density)


def conv_from(padded, kernel, out_rows, out_cols):
    running = jnp.zeros((out_rows, out_cols, padded.shape[2]), jnp.float32)
    for row_off in range(7):
        for col_off in range(7):
            running = (
                running
                + kernel[row_off, col_off]
                * padded[row_off : row_off + out_rows, col_off : col_off + out_cols]
            )
    return running


def conv_back(padded_grad, kernel, out_rows, out_cols):
    running = jnp.zeros((out_rows, out_cols, padded_grad.shape[2]), jnp.float32)
    for row_off in range(7):
        for col_off in range(7):
            running = (
                running
                + kernel[row_off, col_off]
                * padded_grad[
                    6 - row_off : 6 - row_off + out_rows, 6 - col_off : 6 - col_off + out_cols
                ]
            )
    return running


def kernel_grad(grad_z, padded_in):
    out_rows, out_cols = (grad_z.shape[0], grad_z.shape[1])
    kernel_taps = []
    for row_off in range(7):
        for col_off in range(7):
            kernel_taps.append(
                jnp.sum(
                    grad_z * padded_in[row_off : row_off + out_rows, col_off : col_off + out_cols],
                    axis=(0, 1),
                )
            )
    return jnp.stack(kernel_taps).reshape(7, 7, grad_z.shape[2])


def norm_fwd(source, gain, shift):
    center = source - jnp.mean(source, axis=-1, keepdims=True)
    inv_std = lax.rsqrt(jnp.mean(center * center, axis=-1, keepdims=True) + EPSILON)
    norm_hat = center * inv_std
    return (norm_hat, inv_std, (norm_hat * gain + shift).astype(jnp.bfloat16))


def norm_back(grad_n, norm_hat, inv_std, gain):
    scaled = grad_n * gain
    return inv_std * (
        scaled
        - jnp.mean(scaled, axis=-1, keepdims=True)
        - norm_hat * jnp.mean(scaled * norm_hat, axis=-1, keepdims=True)
    )


def mlp_hidden(normed_flat, weight_in, bias_in):
    pre_act = jnp.dot(normed_flat, weight_in, preferred_element_type=jnp.float32) + bias_in
    activation, gelu_slope = gelu_parts(pre_act)
    return (activation.astype(jnp.bfloat16), gelu_slope)


def mlp_forward(normed_flat, weight_in, bias_in, weight_out):
    act_b, gelu_slope = mlp_hidden(normed_flat, weight_in, bias_in)
    mixed = lax.dot_general(
        act_b, weight_out, (((1,), (1,)), ((), ())), preferred_element_type=jnp.float32
    )
    return (act_b, gelu_slope, mixed)


def input_rim(source):
    return with_halo(source, (("rows", 0), ("cols", 1)), 3)


def layer_back(
    grad_b,
    normed_flat,
    act_b,
    gelu_slope,
    norm_hat,
    inv_std,
    kernel,
    gain,
    weight_in,
    weight_out,
    padded_in,
):
    tile_rows, tile_cols, channels = grad_b.shape
    grad_flat = grad_b.reshape(-1, channels)
    grad_wo = lax.dot_general(
        grad_flat, act_b, (((0,), (0,)), ((), ())), preferred_element_type=jnp.float32
    )
    grad_pre = jnp.dot(grad_flat, weight_out, preferred_element_type=jnp.float32) * gelu_slope
    grad_preb = grad_pre.astype(jnp.bfloat16)
    grad_wi = lax.dot_general(
        normed_flat, grad_preb, (((0,), (0,)), ((), ())), preferred_element_type=jnp.float32
    )
    grad_bias = jnp.sum(grad_pre, axis=0)
    grad_n = lax.dot_general(
        grad_preb, weight_in, (((1,), (1,)), ((), ())), preferred_element_type=jnp.float32
    ).reshape(grad_b.shape)
    grad_gain = jnp.sum(grad_n * norm_hat, axis=(0, 1))
    grad_shift = jnp.sum(grad_n, axis=(0, 1))
    grad_z = norm_back(grad_n, norm_hat, inv_std, gain).astype(jnp.bfloat16)
    padded_grad = with_halo(grad_z, (("rows", 0), ("cols", 1)), 3)
    kernel_taps = kernel_grad(grad_z.astype(jnp.float32), padded_in)
    spread = conv_back(padded_grad.astype(jnp.float32), kernel, tile_rows, tile_cols)
    return (spread, kernel_taps, grad_gain, grad_shift, grad_bias, grad_wi, grad_wo)


def shards(activations, grad_out, kernels, norm_gains, norm_shifts, w_in, b_in, w_out):
    tile_rows, tile_cols, channels = activations.shape
    grad_scale = 1.0 / math.sqrt(
        tile_rows * tile_cols * lax.axis_size("rows") * lax.axis_size("cols")
    )
    padded_in = input_rim(activations).astype(jnp.float32)
    conv_one = conv_from(padded_in, kernels[0], tile_rows, tile_cols)
    hat_one, inv_one, normed_grid = norm_fwd(conv_one, norm_gains[0], norm_shifts[0])
    normed_one = normed_grid.reshape(-1, channels)
    act_one, slope_one, mixed_one = mlp_forward(normed_one, w_in[0], b_in[0], w_out[0])
    middle = (activations.astype(jnp.float32) + mixed_one.reshape(activations.shape)).astype(
        jnp.bfloat16
    )
    padded_mid = input_rim(middle)
    padded_mid_wide = padded_mid.astype(jnp.float32)
    conv_two = conv_from(padded_mid_wide, kernels[1], tile_rows, tile_cols)
    hat_two, inv_two, normed_grid_two = norm_fwd(conv_two, norm_gains[1], norm_shifts[1])
    normed_two = normed_grid_two.reshape(-1, channels)
    act_two, slope_two = mlp_hidden(normed_two, w_in[1], b_in[1])
    back_two = layer_back(
        grad_out,
        normed_two,
        act_two,
        slope_two,
        hat_two,
        inv_two,
        kernels[1],
        norm_gains[1],
        w_in[1],
        w_out[1],
        padded_mid_wide,
    )
    grad_mid = (grad_out.astype(jnp.float32) + back_two[0]).astype(jnp.bfloat16)
    back_one = layer_back(
        grad_mid,
        normed_one,
        act_one,
        slope_one,
        hat_one,
        inv_one,
        kernels[0],
        norm_gains[0],
        w_in[0],
        w_out[0],
        padded_in,
    )
    grad_in = (grad_mid.astype(jnp.float32) + back_one[0]).astype(jnp.bfloat16)
    grad_kernels, grad_gains, grad_shifts, grad_b_in = lax.psum(
        (
            jnp.stack([back_one[1], back_two[1]]) * grad_scale,
            jnp.stack([back_one[2], back_two[2]]) * grad_scale,
            jnp.stack([back_one[3], back_two[3]]) * grad_scale,
            jnp.stack([back_one[4], back_two[4]]) * grad_scale,
        ),
        ("rows", "cols"),
    )
    stacked_in = jnp.stack([back_one[5], back_two[5]]) * grad_scale
    stacked_out = jnp.stack([back_one[6], back_two[6]]) * grad_scale
    grad_w_in, grad_w_out = (
        lax.psum_scatter(stacked_in, ("rows", "cols"), scatter_dimension=2, tiled=True),
        lax.psum_scatter(stacked_out, ("rows", "cols"), scatter_dimension=2, tiled=True),
    )
    return (grad_in, grad_kernels, grad_gains, grad_shifts, grad_b_in, grad_w_in, grad_w_out)


def solution(mesh):
    return jax.shard_map(
        shards,
        mesh=mesh,
        in_specs=(P("rows", "cols", None), P("rows", "cols", None), P(), P(), P(), P(), P(), P()),
        out_specs=(
            P("rows", "cols", None),
            P(),
            P(),
            P(),
            P(),
            P(None, None, ("rows", "cols")),
            P(None, None, ("rows", "cols")),
        ),
        check_vma=False,
    )
```

profile of v0, /device:TPU:8, one launch (start us, length us, event | category | flops | bytes accessed | tf_op | source)
XLA Modules:
  0.0 460.9 jit_solution(10851110256736545179)
XLA Ops:
  8.0 6.4 %collective-permute-start.1 = (bf16[3,16,384]{2,1,0:T(8,128)(2,1)S(1)}, bf16[3,16,384]{2,1,0:T(8,128)(2,1)S(1)}, u32[]{:S(2)}, u32[]{:S(2)}) collective-permute-start(bf16[3,16,384]{2,1,0:T(8,128)(2,1)S(1)} %get-tuple-element.268), channel_id=1, source_target_pairs={{16,0},{32,16},{48,32},{64,48},{80,64},{96,80},{112,96},{128,112},... | collective-permute-start | bytes 110600 | tf_op jit(solution)/shard_map/ppermute | solution.py:20
  14.5 1.9 collective-permute-start
  20.3 2.7 collective-permute-done
  27.3 5.9 %collective-permute-done.3 = bf16[22,3,384]{2,1,0:T(4,128)(2,1)S(1)} collective-permute-done((bf16[22,3,384]{2,1,0:T(4,128)(2,1)S(1)}, bf16[22,3,384]{2,1,0:T(4,128)(2,1)S(1)}, u32[]{:S(2)}, u32[]{:S(2)}) %collective-permute-start.3) | collective-permute-done | bytes 50720 | tf_op jit(solution)/shard_map/ppermute | solution.py:20
  33.4 3.8 fusion.226
  38.6 1.8 multiply_convert_fusion.1
  41.6 1.9 collective-permute-start.4
  43.5 6.6 %collective-permute-start.5 = (bf16[3,16,384]{2,1,0:T(8,128)(2,1)S(1)}, bf16[3,16,384]{2,1,0:T(8,128)(2,1)S(1)}, u32[]{:S(2)}, u32[]{:S(2)}) collective-permute-start(bf16[3,16,384]{2,1,0:T(8,128)(2,1)S(1)} %get-tuple-element.267), channel_id=1, source_target_pairs={{16,0},{32,16},{48,32},{64,48},{80,64},{96,80},{112,96},{128,112},... | collective-permute-start | bytes 110600 | tf_op jit(solution)/shard_map/ppermute | solution.py:20
  51.8 7.6 %collective-permute-start.6 = (bf16[22,3,384]{2,1,0:T(4,128)(2,1)S(1)}, bf16[22,3,384]{2,1,0:T(4,128)(2,1)S(1)}, u32[]{:S(2)}, u32[]{:S(2)}) collective-permute-start(bf16[22,3,384]{2,1,0:T(4,128)(2,1)S(1)} %get-tuple-element.258), channel_id=1, source_target_pairs={{0,1},{1,2},{2,3},{3,4},{4,5},{5,6},{6,7},{7,8},{8,9},{9,10},{10,1... | collective-permute-start | bytes 152072 | tf_op jit(solution)/shard_map/ppermute | solution.py:17
  61.0 2.3 collective-permute-done.7
  63.4 3.6 fusion.225
  73.6 1.9 collective-permute-start.8
  75.5 7.1 %collective-permute-start.9 = (bf16[3,16,384]{2,1,0:T(8,128)(2,1)S(1)}, bf16[3,16,384]{2,1,0:T(8,128)(2,1)S(1)}, u32[]{:S(2)}, u32[]{:S(2)}) collective-permute-start(bf16[3,16,384]{2,1,0:T(8,128)(2,1)S(1)} %get-tuple-element.265), channel_id=1, source_target_pairs={{16,0},{32,16},{48,32},{64,48},{80,64},{96,80},{112,96},{128,112},... | collective-permute-start | bytes 110600 | tf_op jit(solution)/shard_map/ppermute | solution.py:20
  82.6 2.0 convolution_bitcast_fusion
  85.4 9.1 %collective-permute-start.10 = (bf16[22,3,384]{2,1,0:T(4,128)(2,1)}, bf16[22,3,384]{2,1,0:T(4,128)(2,1)}, u32[]{:S(2)}, u32[]{:S(2)}) collective-permute-start(bf16[22,3,384]{2,1,0:T(4,128)(2,1)} %get-tuple-element.256), channel_id=1, source_target_pairs={{0,1},{1,2},{2,3},{3,4},{4,5},{5,6},{6,7},{7,8},{8,9},{9,10},{10,1... | collective-permute-start | bytes 152072 | tf_op jit(solution)/shard_map/ppermute | solution.py:17
  112.5 4.3 stack.447
  118.0 3.9 fusion.177
  123.7 1.9 multiply_reduce_fusion.1
  125.7 1.5 fusion.74
  128.9 1.9 convolution_bitcast_fusion.1
  130.8 1.9 convolution_bitcast_fusion.3
  133.5 5.0 %maximum_multiply_fusion.1 = f32[2,384,1536]{2,1,0:T(8,128)} fusion(f32[1,384,1536]{2,1,0:T(8,128)} %convolution_bitcast_fusion, f32[1,384,1536]{2,1,0:T(8,128)} %convolution_bitcast_fusion.1), kind=kLoop, calls=%fused_computation.99 | loop fusion | flops 2359296 | bytes 9437184 | tf_op jit(solution)/shard_map/mul | solution.py:198
  138.5 8.2 %copy.28 = f32[2,384,1536]{1,0,2:T(2,128)} copy(f32[2,384,1536]{2,1,0:T(8,128)} %maximum_multiply_fusion.1) | data formatting | bytes 9437184 | tf_op jit(solution)/shard_map/mul | solution.py:198
  146.6 4.5 maximum_multiply_fusion
  151.1 8.2 %copy.26 = f32[2,384,1536]{1,0,2:T(2,128)} copy(f32[2,384,1536]{2,1,0:T(8,128)} %maximum_multiply_fusion) | data formatting | bytes 9437184 | tf_op jit(solution)/shard_map/mul | solution.py:197
  162.7 2.0 collective-permute-start.12
  164.7 6.6 %collective-permute-start.13 = (bf16[3,16,384]{2,1,0:T(8,128)(2,1)S(1)}, bf16[3,16,384]{2,1,0:T(8,128)(2,1)S(1)}, u32[]{:S(2)}, u32[]{:S(2)}) collective-permute-start(bf16[3,16,384]{2,1,0:T(8,128)(2,1)S(1)} %get-tuple-element.263), channel_id=1, source_target_pairs={{16,0},{32,16},{48,32},{64,48},{80,64},{96,80},{112,96},{128,112},... | collective-permute-start | bytes 110600 | tf_op jit(solution)/shard_map/ppermute | solution.py:20
  173.1 1.9 collective-permute-start.14
  176.3 88.6 %all-reduce.2 = (f32[2,384]{1,0:T(2,128)}, f32[2,384]{1,0:T(2,128)}, f32[2,1536]{1,0:T(2,128)}) all-reduce(f32[2,384]{1,0:T(2,128)S(1)} %maximum_multiply_fusion.4, f32[2,384]{1,0:T(2,128)S(1)} %maximum_multiply_fusion.5, f32[2,1536]{1,0:T(2,128)S(1)} %maximum_multiply_fusion.3), channel_id=1, replica_groups=mesh['rows'=16,'cols'=16] {'rows','cols'}, use_global_device_ids=true, to_apply=%region_109.0 | all-reduce | flops 4608 | bytes 36864 | tf_op jit(solution)/shard_map/psum | solution.py:188
  265.4 4.2 fusion.127
  269.6 180.2 %all-reduce.6.cloned.1.call-done = (f32[2,7,7,384]{3,2,1,0:T(8,128)}, f32[2,384,1536]{1,0,2:T(2,128)}, f32[2,384,1536]{1,0,2:T(2,128)}) async-done(((f32[2,7,7,384]{3,2,1,0:T(8,128)}, f32[2,384,1536]{1,0,2:T(2,128)}, f32[2,384,1536]{1,0,2:T(2,128)}), (f32[2,7,7,384]{3,2,1,0:T(8,128)}, f32[2,384,1536]{1,0,2:T(2,128)}, f32[2,384,1536]{1,0,2:T(2,128)})) %all-reduce.6.cloned.1.call-update) | async-done | bytes 9587728 | tf_op jit(solution)/shard_map/psum | solution.py:188
  449.8 1.7 copy.29
  (433 shorter events, 53.1 us)
Async XLA Ops:
  7.2 442.6 %all-reduce.6.cloned.1.call-start = ((), (), s32[]{:S(2)}) async-start(), calls=%async_computation | async-start | bytes 19218432 | tf_op jit(solution)/shard_map/psum | solution.py:188
  8.0 15.9 %collective-permute-start.1 = (bf16[3,16,384]{2,1,0:T(8,128)(2,1)S(1)}, bf16[3,16,384]{2,1,0:T(8,128)(2,1)S(1)}, u32[]{:S(2)}, u32[]{:S(2)}) collective-permute-start(bf16[3,16,384]{2,1,0:T(8,128)(2,1)S(1)} %get-tuple-element.268), channel_id=1, source_target_pairs={{16,0},{32,16},{48,32},{64,48},{80,64},{96,80},{112,96},{128,112},... | collective-permute-start | bytes 110600 | tf_op jit(solution)/shard_map/ppermute | solution.py:20
  14.5 8.5 %collective-permute-start = (bf16[3,16,384]{2,1,0:T(8,128)(2,1)S(1)}, bf16[3,16,384]{2,1,0:T(8,128)(2,1)S(1)}, u32[]{:S(2)}, u32[]{:S(2)}) collective-permute-start(bf16[3,16,384]{2,1,0:T(8,128)(2,1)S(1)} %get-tuple-element.269), channel_id=1, source_target_pairs={{0,16},{16,32},{32,48},{48,64},{64,80},{80,96},{96,112},{112,128},... | collective-permute-start | bytes 110600 | tf_op jit(solution)/shard_map/ppermute | solution.py:17
  24.1 3.2 collective-permute-start.2
  25.4 7.9 %collective-permute-start.3 = (bf16[22,3,384]{2,1,0:T(4,128)(2,1)S(1)}, bf16[22,3,384]{2,1,0:T(4,128)(2,1)S(1)}, u32[]{:S(2)}, u32[]{:S(2)}) collective-permute-start(bf16[22,3,384]{2,1,0:T(4,128)(2,1)S(1)} %get-tuple-element.261), channel_id=1, source_target_pairs={{1,0},{2,1},{3,2},{4,3},{5,4},{6,5},{7,6},{8,7},{9,8},{10,9},{11,1... | collective-permute-start | bytes 152072 | tf_op jit(solution)/shard_map/ppermute | solution.py:20
  41.6 8.9 %collective-permute-start.4 = (bf16[3,16,384]{2,1,0:T(8,128)(2,1)S(1)}, bf16[3,16,384]{2,1,0:T(8,128)(2,1)S(1)}, u32[]{:S(2)}, u32[]{:S(2)}) collective-permute-start(bf16[3,16,384]{2,1,0:T(8,128)(2,1)S(1)} %get-tuple-element.266), channel_id=1, source_target_pairs={{0,16},{16,32},{32,48},{48,64},{64,80},{80,96},{96,112},{112,128},... | collective-permute-start | bytes 110600 | tf_op jit(solution)/shard_map/ppermute | solution.py:17
  43.5 8.2 %collective-permute-start.5 = (bf16[3,16,384]{2,1,0:T(8,128)(2,1)S(1)}, bf16[3,16,384]{2,1,0:T(8,128)(2,1)S(1)}, u32[]{:S(2)}, u32[]{:S(2)}) collective-permute-start(bf16[3,16,384]{2,1,0:T(8,128)(2,1)S(1)} %get-tuple-element.267), channel_id=1, source_target_pairs={{16,0},{32,16},{48,32},{64,48},{80,64},{96,80},{112,96},{128,112},... | collective-permute-start | bytes 110600 | tf_op jit(solution)/shard_map/ppermute | solution.py:20
  51.8 9.1 %collective-permute-start.6 = (bf16[22,3,384]{2,1,0:T(4,128)(2,1)S(1)}, bf16[22,3,384]{2,1,0:T(4,128)(2,1)S(1)}, u32[]{:S(2)}, u32[]{:S(2)}) collective-permute-start(bf16[22,3,384]{2,1,0:T(4,128)(2,1)S(1)} %get-tuple-element.258), channel_id=1, source_target_pairs={{0,1},{1,2},{2,3},{3,4},{4,5},{5,6},{6,7},{7,8},{8,9},{9,10},{10,1... | collective-permute-start | bytes 152072 | tf_op jit(solution)/shard_map/ppermute | solution.py:17
  59.5 3.8 collective-permute-start.7
  73.6 11.1 %collective-permute-start.8 = (bf16[3,16,384]{2,1,0:T(8,128)(2,1)S(1)}, bf16[3,16,384]{2,1,0:T(8,128)(2,1)S(1)}, u32[]{:S(2)}, u32[]{:S(2)}) collective-permute-start(bf16[3,16,384]{2,1,0:T(8,128)(2,1)S(1)} %get-tuple-element.264), channel_id=1, source_target_pairs={{0,16},{16,32},{32,48},{48,64},{64,80},{80,96},{96,112},{112,128},... | collective-permute-start | bytes 110600 | tf_op jit(solution)/shard_map/ppermute | solution.py:17
  75.5 9.1 %collective-permute-start.9 = (bf16[3,16,384]{2,1,0:T(8,128)(2,1)S(1)}, bf16[3,16,384]{2,1,0:T(8,128)(2,1)S(1)}, u32[]{:S(2)}, u32[]{:S(2)}) collective-permute-start(bf16[3,16,384]{2,1,0:T(8,128)(2,1)S(1)} %get-tuple-element.265), channel_id=1, source_target_pairs={{16,0},{32,16},{48,32},{64,48},{80,64},{96,80},{112,96},{128,112},... | collective-permute-start | bytes 110600 | tf_op jit(solution)/shard_map/ppermute | solution.py:20
  85.4 31.5 %collective-permute-start.10 = (bf16[22,3,384]{2,1,0:T(4,128)(2,1)}, bf16[22,3,384]{2,1,0:T(4,128)(2,1)}, u32[]{:S(2)}, u32[]{:S(2)}) collective-permute-start(bf16[22,3,384]{2,1,0:T(4,128)(2,1)} %get-tuple-element.256), channel_id=1, source_target_pairs={{0,1},{1,2},{2,3},{3,4},{4,5},{5,6},{6,7},{7,8},{8,9},{9,10},{10,1... | collective-permute-start | bytes 152072 | tf_op jit(solution)/shard_map/ppermute | solution.py:17
  94.5 22.4 %collective-permute-start.11 = (bf16[22,3,384]{2,1,0:T(4,128)(2,1)}, bf16[22,3,384]{2,1,0:T(4,128)(2,1)}, u32[]{:S(2)}, u32[]{:S(2)}) collective-permute-start(bf16[22,3,384]{2,1,0:T(4,128)(2,1)} %get-tuple-element.257), channel_id=1, source_target_pairs={{1,0},{2,1},{3,2},{4,3},{5,4},{6,5},{7,6},{8,7},{9,8},{10,9},{11,1... | collective-permute-start | bytes 152072 | tf_op jit(solution)/shard_map/ppermute | solution.py:20
  160.0 105.0 %copy-start.3 = (bf16[16,16,384]{2,1,0:T(8,128)(2,1)S(1)}, bf16[16,16,384]{2,1,0:T(8,128)(2,1)}, u32[]{:S(2)}) copy-start(bf16[16,16,384]{2,1,0:T(8,128)(2,1)} %copy-done.2) | copy-start | bytes 589828
  160.0 105.0 %copy-start.15 = (f32[384]{0:T(512)S(1)}, f32[384]{0:T(512)}, u32[]{:S(2)}) copy-start(f32[384]{0:T(512)} %copy-done.14) | copy-start | bytes 4612
  160.0 105.0 %copy-start.17 = (f32[384]{0:T(512)S(1)}, f32[384]{0:T(512)}, u32[]{:S(2)}) copy-start(f32[384]{0:T(512)} %copy-done.16) | copy-start | bytes 4612
  160.0 105.0 %copy-start.19 = (f32[384]{0:T(512)S(1)}, f32[384]{0:T(512)}, u32[]{:S(2)}) copy-start(f32[384]{0:T(512)} %copy-done.18) | copy-start | bytes 4612
  160.1 105.0 %copy-start.21 = (f32[384]{0:T(512)S(1)}, f32[384]{0:T(512)}, u32[]{:S(2)}) copy-start(f32[384]{0:T(512)} %copy-done.20) | copy-start | bytes 4612
  160.1 105.0 %copy-start.23 = (f32[384]{0:T(512)S(1)}, f32[384]{0:T(512)}, u32[]{:S(2)}) copy-start(f32[384]{0:T(512)} %copy-done.22) | copy-start | bytes 4612
  160.1 105.0 %copy-start.25 = (f32[384]{0:T(512)S(1)}, f32[384]{0:T(512)}, u32[]{:S(2)}) copy-start(f32[384]{0:T(512)} %copy-done.24) | copy-start | bytes 4612
  160.1 105.0 %copy-start.27 = (f32[384]{0:T(512)S(1)}, f32[384]{0:T(512)}, u32[]{:S(2)}) copy-start(f32[384]{0:T(512)} %copy-done.26) | copy-start | bytes 4612
  160.1 105.0 %copy-start.29 = (f32[384]{0:T(512)S(1)}, f32[384]{0:T(512)}, u32[]{:S(2)}) copy-start(f32[384]{0:T(512)} %copy-done.28) | copy-start | bytes 4612
  160.1 105.0 %copy-start.31 = (f32[384]{0:T(512)S(1)}, f32[384]{0:T(512)}, u32[]{:S(2)}) copy-start(f32[384]{0:T(512)} %copy-done.30) | copy-start | bytes 4612
  160.1 105.0 %copy-start.33 = (f32[384]{0:T(512)S(1)}, f32[384]{0:T(512)}, u32[]{:S(2)}) copy-start(f32[384]{0:T(512)} %copy-done.32) | copy-start | bytes 4612
  160.1 105.0 %copy-start.35 = (f32[384]{0:T(512)S(1)}, f32[384]{0:T(512)}, u32[]{:S(2)}) copy-start(f32[384]{0:T(512)} %copy-done.34) | copy-start | bytes 4612
  160.1 105.0 %copy-start.37 = (f32[384]{0:T(512)S(1)}, f32[384]{0:T(512)}, u32[]{:S(2)}) copy-start(f32[384]{0:T(512)} %copy-done.36) | copy-start | bytes 4612
  160.1 105.0 %copy-start.39 = (f32[384]{0:T(512)S(1)}, f32[384]{0:T(512)}, u32[]{:S(2)}) copy-start(f32[384]{0:T(512)} %copy-done.38) | copy-start | bytes 4612
  160.2 105.0 %copy-start.41 = (f32[384]{0:T(512)S(1)}, f32[384]{0:T(512)}, u32[]{:S(2)}) copy-start(f32[384]{0:T(512)} %copy-done.40) | copy-start | bytes 4612
  162.7 9.3 %collective-permute-start.12 = (bf16[3,16,384]{2,1,0:T(8,128)(2,1)S(1)}, bf16[3,16,384]{2,1,0:T(8,128)(2,1)S(1)}, u32[]{:S(2)}, u32[]{:S(2)}) collective-permute-start(bf16[3,16,384]{2,1,0:T(8,128)(2,1)S(1)} %get-tuple-element.262), channel_id=1, source_target_pairs={{0,16},{16,32},{32,48},{48,64},{64,80},{80,96},{96,112},{112,128},... | collective-permute-start | bytes 110600 | tf_op jit(solution)/shard_map/ppermute | solution.py:17
  164.7 8.3 %collective-permute-start.13 = (bf16[3,16,384]{2,1,0:T(8,128)(2,1)S(1)}, bf16[3,16,384]{2,1,0:T(8,128)(2,1)S(1)}, u32[]{:S(2)}, u32[]{:S(2)}) collective-permute-start(bf16[3,16,384]{2,1,0:T(8,128)(2,1)S(1)} %get-tuple-element.263), channel_id=1, source_target_pairs={{16,0},{32,16},{48,32},{64,48},{80,64},{96,80},{112,96},{128,112},... | collective-permute-start | bytes 110600 | tf_op jit(solution)/shard_map/ppermute | solution.py:20
  173.1 91.8 %collective-permute-start.14 = (bf16[22,3,384]{2,1,0:T(4,128)(2,1)S(1)}, bf16[22,3,384]{2,1,0:T(4,128)(2,1)S(1)}, u32[]{:S(2)}, u32[]{:S(2)}) collective-permute-start(bf16[22,3,384]{2,1,0:T(4,128)(2,1)S(1)} %get-tuple-element.254), channel_id=1, source_target_pairs={{0,1},{1,2},{2,3},{3,4},{4,5},{5,6},{6,7},{7,8},{8,9},{9,10},{10,1... | collective-permute-start | bytes 152072 | tf_op jit(solution)/shard_map/ppermute | solution.py:17
  175.0 89.9 %collective-permute-start.15 = (bf16[22,3,384]{2,1,0:T(4,128)(2,1)S(1)}, bf16[22,3,384]{2,1,0:T(4,128)(2,1)S(1)}, u32[]{:S(2)}, u32[]{:S(2)}) collective-permute-start(bf16[22,3,384]{2,1,0:T(4,128)(2,1)S(1)} %get-tuple-element.255), channel_id=1, source_target_pairs={{1,0},{2,1},{3,2},{4,3},{5,4},{6,5},{7,6},{8,7},{9,8},{10,9},{11,1... | collective-permute-start | bytes 152072 | tf_op jit(solution)/shard_map/ppermute | solution.py:20
  (111 other events, 3747.5 us)
Sparse Core Ops, SparseCore 0:
  160.1 289.5 all-reduce.5
where the time goes:
time: 463 us; the launch traced here: 461 us
  waiting for transfers between devices  193 us (42%)
  blocking collectives  88.6 us (19%)
  starting transfers between devices  59.6 us (13%)
  local copies, waits for them, and re-layouts  53.2 us (11%)
  other arithmetic  34.6 us (7%)
  between operations  16.7 us (4%)
  matrix products  14.8 us (3%)
    psum x1, waiting for transfers between devices, shards(): lax.psum((jnp.stack([back_one[1], back_two[1]]) * grad_scale, jnp.stack([...  180 us
    psum x1, blocking collectives, shards(): lax.psum((jnp.stack([back_one[1], back_two[1]]) * grad_scale, jnp.stack([...  88.6 us
    ppermute x8, starting transfers between devices, with_halo(): lax.ppermute(lax.slice_in_dim(block, 0, width, axis=dim), axis, backward)  31.9 us
    ppermute x8, starting transfers between devices, with_halo(): lax.ppermute(lax.slice_in_dim(block, block.shape[dim] - width, None, axis...  27.7 us
    another operation x100, local copies, waits for them, and re-layouts, kernel_grad(): return jnp.stack(kernel_taps).reshape(7, 7, grad_z.shape[2])  20.7 us
    ppermute x8, waiting for transfers between devices, with_halo(): lax.ppermute(lax.slice_in_dim(block, 0, width, axis=dim), axis, backward)  10.5 us
  transfers between devices with their start and end apart: 17, of which 6 were waited for; matrix products, arithmetic and copies ran while one was open for 8% of the time, Pallas kernels for 0%

commit v1 on v0

--- a/solution.py
+++ b/solution.py
@@ -7,6 +7,11 @@
 EPSILON = 1e-06
 ROOT_HALF = 0.7071067811865476
 INV_ROOT_TAU = 0.3989422804014327
+
+
+def one_after_other(x, first, second):
+    partial = lax.psum(x, first)
+    return lax.psum(partial, second)
 
 
 def with_halo(block, sides, width):
@@ -185,14 +190,15 @@
         padded_in,
     )
     grad_in = (grad_mid.astype(jnp.float32) + back_one[0]).astype(jnp.bfloat16)
-    grad_kernels, grad_gains, grad_shifts, grad_b_in = lax.psum(
+    grad_kernels, grad_gains, grad_shifts, grad_b_in = one_after_other(
         (
             jnp.stack([back_one[1], back_two[1]]) * grad_scale,
             jnp.stack([back_one[2], back_two[2]]) * grad_scale,
             jnp.stack([back_one[3], back_two[3]]) * grad_scale,
             jnp.stack([back_one[4], back_two[4]]) * grad_scale,
         ),
-        ("rows", "cols"),
+        "cols",
+        "rows",
     )
     stacked_in = jnp.stack([back_one[5], back_two[5]]) * grad_scale
     stacked_out = jnp.stack([back_one[6], back_two[6]]) * grad_scale

time: 463 us -> 756 us (1.63)
  waiting for transfers between devices: 193 us -> 425 us
  blocking collectives: 88.6 us -> 154 us
    unnamed x1 -> x4, waiting for transfers between devices: 0.02 us -> 238 us
    psum x1 -> x2, blocking collectives: 88.6 us -> 154 us  [the longest x1 85.2 us: one_after_other(): partial = lax.psum(x, first)]
    ppermute x8, waiting for transfers between devices: 2.76 us -> 15 us  [with_halo(): lax.ppermute(lax.slice_in_dim(block, block.shape[dim] - width, None, axis...]
    ppermute x8, starting transfers between devices: 31.9 us -> 20.9 us  [with_halo(): lax.ppermute(lax.slice_in_dim(block, 0, width, axis=dim), axis, backward)]
    ppermute x8, waiting for transfers between devices: 10.5 us -> 0.02 us  [with_halo(): lax.ppermute(lax.slice_in_dim(block, 0, width, axis=dim), axis, backward)]
    ppermute x8, starting transfers between devices: 27.7 us -> 36.2 us  [with_halo(): lax.ppermute(lax.slice_in_dim(block, block.shape[dim] - width, None, axis...]
    psum x1 -> x2, waiting for transfers between devices: 180 us -> 173 us  [the longest x1 173 us: one_after_other(): partial = lax.psum(x, first)]
  transfers between devices with their start and end apart: 17 -> 19, of which waited for: 6 -> 7; matrix products, arithmetic and copies ran while one was open for 8% -> 8% of each run, Pallas kernels for 0% -> 0%
where the time goes in v1:
time: 756 us; the launch traced here: 754 us
  waiting for transfers between devices  425 us (56%)
  blocking collectives  154 us (20%)
  starting transfers between devices  57.3 us (8%)
  local copies, waits for them, and re-layouts  52.3 us (7%)
  other arithmetic  34.3 us (5%)
  between operations  16.5 us (2%)
  matrix products  13.4 us (2%)
    unnamed x4, waiting for transfers between devices  238 us
    psum x1, waiting for transfers between devices, one_after_other(): partial = lax.psum(x, first)  173 us
    psum x1, blocking collectives, one_after_other(): partial = lax.psum(x, first)  85.2 us
    psum x1, blocking collectives, one_after_other(): return lax.psum(partial, second)  69.2 us
    ppermute x8, starting transfers between devices, with_halo(): lax.ppermute(lax.slice_in_dim(block, block.shape[dim] - width, None, axis...  36.2 us
    ppermute x8, starting transfers between devices, with_halo(): lax.ppermute(lax.slice_in_dim(block, 0, width, axis=dim), axis, backward)  20.9 us
    another operation x100, local copies, waits for them, and re-layouts, kernel_grad(): return jnp.stack(kernel_taps).reshape(7, 7, grad_z.shape[2])  20.3 us
  transfers between devices with their start and end apart: 19, of which 7 were waited for; matrix products, arithmetic and copies ran while one was open for 8% of the time, Pallas kernels for 0%

profile of v1, /device:TPU:8, one launch (start us, length us, event | category | flops | bytes accessed | tf_op | source)
XLA Modules:
  0.0 753.6 jit_solution(15610306557100083586)
XLA Ops:
  8.0 3.8 collective-permute-start
  11.9 4.7 collective-permute-start.1
  22.9 3.0 collective-permute-start.2
  27.0 3.8 fusion.226
  32.2 1.8 multiply_convert_fusion.1
  35.2 3.7 collective-permute-start.5
  38.9 2.1 collective-permute-start.4
  41.3 6.3 collective-permute-done.4
  49.0 8.0 %collective-permute-start.6 = (bf16[22,3,384]{2,1,0:T(4,128)(2,1)S(1)}, bf16[22,3,384]{2,1,0:T(4,128)(2,1)S(1)}, u32[]{:S(2)}, u32[]{:S(2)}) collective-permute-start(bf16[22,3,384]{2,1,0:T(4,128)(2,1)S(1)} %get-tuple-element.260), channel_id=1, source_target_pairs={{0,1},{1,2},{2,3},{3,4},{4,5},{5,6},{6,7},{7,8},{8,9},{9,10},{10,1... | collective-permute-start | bytes 152072 | tf_op jit(solution)/shard_map/ppermute | solution.py:22
  58.1 3.6 fusion.225
  68.3 1.9 collective-permute-start.9
  70.2 4.1 collective-permute-start.8
  74.3 2.0 convolution_bitcast_fusion
  76.3 2.4 collective-permute-done.8
  80.8 10.2 %collective-permute-start.10 = (bf16[22,3,384]{2,1,0:T(4,128)(2,1)}, bf16[22,3,384]{2,1,0:T(4,128)(2,1)}, u32[]{:S(2)}, u32[]{:S(2)}) collective-permute-start(bf16[22,3,384]{2,1,0:T(4,128)(2,1)} %get-tuple-element.258), channel_id=1, source_target_pairs={{0,1},{1,2},{2,3},{3,4},{4,5},{5,6},{6,7},{7,8},{8,9},{9,10},{10,1... | collective-permute-start | bytes 152072 | tf_op jit(solution)/shard_map/ppermute | solution.py:22
  107.9 3.6 stack.447
  112.7 3.9 fusion.177
  118.5 1.9 multiply_reduce_fusion.1
  123.5 1.9 convolution_bitcast_fusion.3
  126.9 4.5 maximum_multiply_fusion
  131.9 172.8 %all-reduce.9.cloned.1.call-done = f32[2,7,7,384]{3,2,1,0:T(8,128)} async-done(((f32[2,7,7,384]{3,2,1,0:T(8,128)}), f32[2,7,7,384]{3,2,1,0:T(8,128)}) %all-reduce.9.cloned.1.call-update) | async-done | bytes 150544 | tf_op jit(solution)/shard_map/psum | solution.py:13
  304.8 4.7 maximum_multiply_fusion.1
  309.6 8.2 %copy.26 = f32[2,384,1536]{1,0,2:T(2,128)} copy(f32[2,384,1536]{2,1,0:T(8,128)} %maximum_multiply_fusion) | data formatting | bytes 9437184 | tf_op jit(solution)/shard_map/mul | solution.py:203
  317.7 8.2 %copy.28 = f32[2,384,1536]{1,0,2:T(2,128)} copy(f32[2,384,1536]{2,1,0:T(8,128)} %maximum_multiply_fusion.1) | data formatting | bytes 9437184 | tf_op jit(solution)/shard_map/mul | solution.py:204
  327.7 5.4 collective-permute-start.13
  333.1 1.9 collective-permute-start.12
  336.5 5.2 collective-permute-done.12
  343.1 3.0 collective-permute-start.14
  346.1 85.2 %all-reduce.3 = (f32[2,384]{1,0:T(2,128)S(1)}, f32[2,384]{1,0:T(2,128)S(1)}, f32[2,1536]{1,0:T(2,128)S(1)}) all-reduce(f32[2,384]{1,0:T(2,128)S(1)} %maximum_multiply_fusion.4, f32[2,384]{1,0:T(2,128)S(1)} %maximum_multiply_fusion.5, f32[2,1536]{1,0:T(2,128)S(1)} %maximum_multiply_fusion.3), channel_id=1, replica_groups=mesh['rows'=16,'cols'=16] {'cols'}, use_global_device_ids=true, to_apply=%region_110.0 | all-reduce | flops 4608 | bytes 36864 | tf_op jit(solution)/shard_map/psum | solution.py:13
  431.4 69.2 %all-reduce.4 = (f32[2,384]{1,0:T(2,128)}, f32[2,384]{1,0:T(2,128)}, f32[2,1536]{1,0:T(2,128)}) all-reduce(f32[2,384]{1,0:T(2,128)S(1)} %get-tuple-element.240, f32[2,384]{1,0:T(2,128)S(1)} %get-tuple-element.241, f32[2,1536]{1,0:T(2,128)S(1)} %get-tuple-element.242), channel_id=1, replica_groups=mesh['rows'=16,'cols'=16] {'rows'}, use_global_device_ids=true, to_apply=%region_111.0 | all-reduce | flops 4608 | bytes 36864 | tf_op jit(solution)/shard_map/psum | solution.py:14
  501.2 4.1 fusion.127
  506.9 237.5 %all-reduce.13.cloned.1.call-done = (f32[2,384,1536]{1,0,2:T(2,128)}, f32[2,384,1536]{1,0,2:T(2,128)}) async-done(((f32[2,384,1536]{1,0,2:T(2,128)}, f32[2,384,1536]{1,0,2:T(2,128)}), (f32[2,384,1536]{1,0,2:T(2,128)}, f32[2,384,1536]{1,0,2:T(2,128)})) %all-reduce.13.cloned.1.call-update) | async-done | bytes 9437200
  (442 shorter events, 54.1 us)
Async XLA Ops:
  7.2 297.6 %all-reduce.9.cloned.1.call-start = ((), (), s32[]{:S(2)}) async-start(), calls=%async_computation | async-start | bytes 344064 | tf_op jit(solution)/shard_map/psum | solution.py:13
  8.0 12.5 %collective-permute-start = (bf16[3,16,384]{2,1,0:T(8,128)(2,1)S(1)}, bf16[3,16,384]{2,1,0:T(8,128)(2,1)S(1)}, u32[]{:S(2)}, u32[]{:S(2)}) collective-permute-start(bf16[3,16,384]{2,1,0:T(8,128)(2,1)S(1)} %get-tuple-element.271), channel_id=1, source_target_pairs={{0,16},{16,32},{32,48},{48,64},{64,80},{80,96},{96,112},{112,128},... | collective-permute-start | bytes 110600 | tf_op jit(solution)/shard_map/ppermute | solution.py:22
  11.9 9.6 %collective-permute-start.1 = (bf16[3,16,384]{2,1,0:T(8,128)(2,1)S(1)}, bf16[3,16,384]{2,1,0:T(8,128)(2,1)S(1)}, u32[]{:S(2)}, u32[]{:S(2)}) collective-permute-start(bf16[3,16,384]{2,1,0:T(8,128)(2,1)S(1)} %get-tuple-element.270), channel_id=1, source_target_pairs={{16,0},{32,16},{48,32},{64,48},{80,64},{96,80},{112,96},{128,112},... | collective-permute-start | bytes 110600 | tf_op jit(solution)/shard_map/ppermute | solution.py:25
  21.6 5.0 collective-permute-start.3
  22.9 3.9 collective-permute-start.2
  35.2 6.2 collective-permute-start.5
  38.9 8.8 %collective-permute-start.4 = (bf16[3,16,384]{2,1,0:T(8,128)(2,1)S(1)}, bf16[3,16,384]{2,1,0:T(8,128)(2,1)S(1)}, u32[]{:S(2)}, u32[]{:S(2)}) collective-permute-start(bf16[3,16,384]{2,1,0:T(8,128)(2,1)S(1)} %get-tuple-element.268), channel_id=1, source_target_pairs={{0,16},{16,32},{32,48},{48,64},{64,80},{80,96},{96,112},{112,128},... | collective-permute-start | bytes 110600 | tf_op jit(solution)/shard_map/ppermute | solution.py:22
  47.7 9.5 %collective-permute-start.7 = (bf16[22,3,384]{2,1,0:T(4,128)(2,1)S(1)}, bf16[22,3,384]{2,1,0:T(4,128)(2,1)S(1)}, u32[]{:S(2)}, u32[]{:S(2)}) collective-permute-start(bf16[22,3,384]{2,1,0:T(4,128)(2,1)S(1)} %get-tuple-element.261), channel_id=1, source_target_pairs={{1,0},{2,1},{3,2},{4,3},{5,4},{6,5},{7,6},{8,7},{9,8},{10,9},{11,1... | collective-permute-start | bytes 152072 | tf_op jit(solution)/shard_map/ppermute | solution.py:25
  49.0 8.9 %collective-permute-start.6 = (bf16[22,3,384]{2,1,0:T(4,128)(2,1)S(1)}, bf16[22,3,384]{2,1,0:T(4,128)(2,1)S(1)}, u32[]{:S(2)}, u32[]{:S(2)}) collective-permute-start(bf16[22,3,384]{2,1,0:T(4,128)(2,1)S(1)} %get-tuple-element.260), channel_id=1, source_target_pairs={{0,1},{1,2},{2,3},{3,4},{4,5},{5,6},{6,7},{7,8},{8,9},{9,10},{10,1... | collective-permute-start | bytes 152072 | tf_op jit(solution)/shard_map/ppermute | solution.py:22
  68.3 8.0 %collective-permute-start.9 = (bf16[3,16,384]{2,1,0:T(8,128)(2,1)S(1)}, bf16[3,16,384]{2,1,0:T(8,128)(2,1)S(1)}, u32[]{:S(2)}, u32[]{:S(2)}) collective-permute-start(bf16[3,16,384]{2,1,0:T(8,128)(2,1)S(1)} %get-tuple-element.267), channel_id=1, source_target_pairs={{16,0},{32,16},{48,32},{64,48},{80,64},{96,80},{112,96},{128,112},... | collective-permute-start | bytes 110600 | tf_op jit(solution)/shard_map/ppermute | solution.py:25
  70.2 8.5 %collective-permute-start.8 = (bf16[3,16,384]{2,1,0:T(8,128)(2,1)S(1)}, bf16[3,16,384]{2,1,0:T(8,128)(2,1)S(1)}, u32[]{:S(2)}, u32[]{:S(2)}) collective-permute-start(bf16[3,16,384]{2,1,0:T(8,128)(2,1)S(1)} %get-tuple-element.266), channel_id=1, source_target_pairs={{0,16},{16,32},{32,48},{48,64},{64,80},{80,96},{96,112},{112,128},... | collective-permute-start | bytes 110600 | tf_op jit(solution)/shard_map/ppermute | solution.py:22
  79.5 32.1 %collective-permute-start.11 = (bf16[22,3,384]{2,1,0:T(4,128)(2,1)}, bf16[22,3,384]{2,1,0:T(4,128)(2,1)}, u32[]{:S(2)}, u32[]{:S(2)}) collective-permute-start(bf16[22,3,384]{2,1,0:T(4,128)(2,1)} %get-tuple-element.259), channel_id=1, source_target_pairs={{1,0},{2,1},{3,2},{4,3},{5,4},{6,5},{7,6},{8,7},{9,8},{10,9},{11,1... | collective-permute-start | bytes 152072 | tf_op jit(solution)/shard_map/ppermute | solution.py:25
  80.8 30.8 %collective-permute-start.10 = (bf16[22,3,384]{2,1,0:T(4,128)(2,1)}, bf16[22,3,384]{2,1,0:T(4,128)(2,1)}, u32[]{:S(2)}, u32[]{:S(2)}) collective-permute-start(bf16[22,3,384]{2,1,0:T(4,128)(2,1)} %get-tuple-element.258), channel_id=1, source_target_pairs={{0,1},{1,2},{2,3},{3,4},{4,5},{5,6},{6,7},{7,8},{8,9},{9,10},{10,1... | collective-permute-start | bytes 152072 | tf_op jit(solution)/shard_map/ppermute | solution.py:22
  126.8 378.4 %all-reduce.11.cloned.1.call-start = ((), (), s32[]{:S(2)}) async-start(), calls=%async_computation.1 | async-start | bytes 344064 | tf_op jit(solution)/shard_map/psum | solution.py:14
  304.8 439.7 %all-reduce.13.cloned.1.call-start = ((), (), s32[]{:S(2)}) async-start(), calls=%async_computation.2 | async-start | bytes 18874368
  325.9 174.9 %copy-start.4 = (bf16[16,16,384]{2,1,0:T(8,128)(2,1)S(1)}, bf16[16,16,384]{2,1,0:T(8,128)(2,1)}, u32[]{:S(2)}) copy-start(bf16[16,16,384]{2,1,0:T(8,128)(2,1)} %copy-done.2) | copy-start | bytes 589828
  325.9 174.9 %copy-start.16 = (f32[384]{0:T(512)S(1)}, f32[384]{0:T(512)}, u32[]{:S(2)}) copy-start(f32[384]{0:T(512)} %copy-done.15) | copy-start | bytes 4612
  325.9 174.9 %copy-start.18 = (f32[384]{0:T(512)S(1)}, f32[384]{0:T(512)}, u32[]{:S(2)}) copy-start(f32[384]{0:T(512)} %copy-done.17) | copy-start | bytes 4612
  325.9 174.9 %copy-start.20 = (f32[384]{0:T(512)S(1)}, f32[384]{0:T(512)}, u32[]{:S(2)}) copy-start(f32[384]{0:T(512)} %copy-done.19) | copy-start | bytes 4612
  326.0 174.9 %copy-start.22 = (f32[384]{0:T(512)S(1)}, f32[384]{0:T(512)}, u32[]{:S(2)}) copy-start(f32[384]{0:T(512)} %copy-done.21) | copy-start | bytes 4612
  326.0 174.9 %copy-start.24 = (f32[384]{0:T(512)S(1)}, f32[384]{0:T(512)}, u32[]{:S(2)}) copy-start(f32[384]{0:T(512)} %copy-done.23) | copy-start | bytes 4612
  326.0 174.9 %copy-start.26 = (f32[384]{0:T(512)S(1)}, f32[384]{0:T(512)}, u32[]{:S(2)}) copy-start(f32[384]{0:T(512)} %copy-done.25) | copy-start | bytes 4612
  326.0 174.9 %copy-start.28 = (f32[384]{0:T(512)S(1)}, f32[384]{0:T(512)}, u32[]{:S(2)}) copy-start(f32[384]{0:T(512)} %copy-done.27) | copy-start | bytes 4612
  326.0 174.9 %copy-start.30 = (f32[384]{0:T(512)S(1)}, f32[384]{0:T(512)}, u32[]{:S(2)}) copy-start(f32[384]{0:T(512)} %copy-done.29) | copy-start | bytes 4612
  326.0 174.9 %copy-start.32 = (f32[384]{0:T(512)S(1)}, f32[384]{0:T(512)}, u32[]{:S(2)}) copy-start(f32[384]{0:T(512)} %copy-done.31) | copy-start | bytes 4612
  326.0 174.9 %copy-start.34 = (f32[384]{0:T(512)S(1)}, f32[384]{0:T(512)}, u32[]{:S(2)}) copy-start(f32[384]{0:T(512)} %copy-done.33) | copy-start | bytes 4612
  326.0 174.9 %copy-start.36 = (f32[384]{0:T(512)S(1)}, f32[384]{0:T(512)}, u32[]{:S(2)}) copy-start(f32[384]{0:T(512)} %copy-done.35) | copy-start | bytes 4612
  326.0 174.9 %copy-start.38 = (f32[384]{0:T(512)S(1)}, f32[384]{0:T(512)}, u32[]{:S(2)}) copy-start(f32[384]{0:T(512)} %copy-done.37) | copy-start | bytes 4612
  327.7 8.8 %collective-permute-start.13 = (bf16[3,16,384]{2,1,0:T(8,128)(2,1)S(1)}, bf16[3,16,384]{2,1,0:T(8,128)(2,1)S(1)}, u32[]{:S(2)}, u32[]{:S(2)}) collective-permute-start(bf16[3,16,384]{2,1,0:T(8,128)(2,1)S(1)} %get-tuple-element.265), channel_id=1, source_target_pairs={{16,0},{32,16},{48,32},{64,48},{80,64},{96,80},{112,96},{128,112},... | collective-permute-start | bytes 110600 | tf_op jit(solution)/shard_map/ppermute | solution.py:25
  333.1 8.6 %collective-permute-start.12 = (bf16[3,16,384]{2,1,0:T(8,128)(2,1)S(1)}, bf16[3,16,384]{2,1,0:T(8,128)(2,1)S(1)}, u32[]{:S(2)}, u32[]{:S(2)}) collective-permute-start(bf16[3,16,384]{2,1,0:T(8,128)(2,1)S(1)} %get-tuple-element.264), channel_id=1, source_target_pairs={{0,16},{16,32},{32,48},{48,64},{64,80},{80,96},{96,112},{112,128},... | collective-permute-start | bytes 110600 | tf_op jit(solution)/shard_map/ppermute | solution.py:22
  341.8 158.8 %collective-permute-start.15 = (bf16[22,3,384]{2,1,0:T(4,128)(2,1)S(1)}, bf16[22,3,384]{2,1,0:T(4,128)(2,1)S(1)}, u32[]{:S(2)}, u32[]{:S(2)}) collective-permute-start(bf16[22,3,384]{2,1,0:T(4,128)(2,1)S(1)} %get-tuple-element.257), channel_id=1, source_target_pairs={{1,0},{2,1},{3,2},{4,3},{5,4},{6,5},{7,6},{8,7},{9,8},{10,9},{11,1... | collective-permute-start | bytes 152072 | tf_op jit(solution)/shard_map/ppermute | solution.py:25
  343.1 157.5 %collective-permute-start.14 = (bf16[22,3,384]{2,1,0:T(4,128)(2,1)S(1)}, bf16[22,3,384]{2,1,0:T(4,128)(2,1)S(1)}, u32[]{:S(2)}, u32[]{:S(2)}) collective-permute-start(bf16[22,3,384]{2,1,0:T(4,128)(2,1)S(1)} %get-tuple-element.256), channel_id=1, source_target_pairs={{0,1},{1,2},{2,3},{3,4},{4,5},{5,6},{6,7},{7,8},{8,9},{9,10},{10,1... | collective-permute-start | bytes 152072 | tf_op jit(solution)/shard_map/ppermute | solution.py:22
  (114 other events, 5565.5 us)
Sparse Core Ops, SparseCore 0:
  127.0 177.7 all-reduce.8
  307.4 152.3 all-reduce.10
  465.5 278.8 all-reduce.12
